TPU v7x, 32 devices: a whole 2x2x4 slice. The times are simulated.
32 devices in a mesh: egrp: 2 (over x), space: 16 (over z, y, core).
Axes of the slice: x: 2, y: 2, z: 4, core: 2. Of those that a mesh axis runs over, the one named last changes fastest.
Arguments:
- dist: float32 [2, 1024, 64, 128], P(None, 'egrp', 'space'), may hold values from -12 to 12
- hist_x: bfloat16 [4, 2, 1024, 64, 128], P(None, None, 'egrp', 'space'), may hold values from -6 to 6
- hist_g: bfloat16 [4, 2, 1024, 64, 128], P(None, None, 'egrp', 'space'), may hold values from -12 to 12
- mobility: float32 [64, 128], P('space'), may hold values from 0.2 to 2
- region: int32 [64, 128], P('space'), may hold values from 0 to 3
- phonon_bins: int32 [4], replicated, may hold values from 48 to 64, as said below
- coupling: float32 [4], replicated, may hold values from 0.2 to 1.5
- hist_used: int32 [2, 4], replicated, may hold values 0 or 1
Outputs:
- drifted: float32 [2, 1024, 64, 128], P(None, 'egrp', 'space')
Inputs may be any that keep to these rules, and one draw needn't show every extreme that they name: `phonon_bins`: each value lies in 48 to 64; both ends occur.
All inputs are finite; a program needn't handle non-finite values.
Results may differ from a plain program's by a relative error of at most 0.0003.
Values sent between devices are 32-bit elements; how exact they have to be, the bound alone decides.
A program may use at most 128 MiB of HBM per device.

v0:
```python
import jax
import jax.numpy as jnp
from jax import lax
from jax.sharding import PartitionSpec as P

NE = 1024
HISTORY = 4
NREGION = 4
KMAX = 64
COLS = 64


def extended(block, sides, width):
    for axis, dim in sides:
        count = lax.axis_size(axis)
        forward = [(i, i + 1) for i in range(count - 1)]
        backward = [(target, source) for source, target in forward]
        low = lax.ppermute(
            lax.slice_in_dim(block, block.shape[dim] - width, None, axis=dim), axis, forward
        )
        high = lax.ppermute(lax.slice_in_dim(block, 0, width, axis=dim), axis, backward)
        block = jnp.concatenate([low, block, high], axis=dim)
    return block


def add_face(total, field, moved, mobility, moved_mob, valid):
    return total + jnp.where(valid, 0.5 * (mobility + moved_mob) * (moved - field), 0.0)


def local(dist, hist_x, hist_g, mobility, region, phonon_bins, coupling, hist_used):
    width = dist.shape[1]
    rows = dist.shape[2]
    cells = dist.shape[3]
    flat_g = hist_g.reshape(HISTORY, 2, -1)
    energy_ids = lax.axis_index("egrp") * width + jnp.arange(width, dtype=jnp.int32)
    dos = jnp.sqrt((energy_ids.astype(jnp.float32) + 0.5) / NE)
    even = dist[0]
    odd = dist[1]
    outrate = jnp.zeros(even.shape, jnp.float32)
    lam = jnp.zeros(region.shape, jnp.float32)
    for index in range(NREGION):
        offset = phonon_bins[index]
        lower = energy_ids - offset
        upper = energy_ids + offset
        dos_low = jnp.where(
            lower >= 0, jnp.sqrt((jnp.maximum(lower, 0).astype(jnp.float32) + 0.5) / NE), 0.0
        )
        dos_high = jnp.where(upper < NE, jnp.sqrt((upper.astype(jnp.float32) + 0.5) / NE), 0.0)
        rate = coupling[index] * (1.5 * dos_low + 0.5 * dos_high)
        outrate = jnp.where((region == index)[None], rate[:, None, None], outrate)
        lam = jnp.where(region == index, coupling[index], lam)
    column = lax.all_to_all(
        even.reshape(width, rows * cells), "egrp", split_axis=1, concat_axis=0, tiled=True
    )
    span = column.shape[1]
    column_region = lax.dynamic_slice_in_dim(
        region.reshape(-1), lax.axis_index("egrp") * span, span
    )
    padded = jnp.pad(column, ((KMAX, KMAX), (0, 0)))
    total = column.shape[0]
    partial_sum = jnp.zeros(column.shape, jnp.float32)
    for index in range(NREGION):
        offset = phonon_bins[index]
        above = lax.dynamic_slice_in_dim(padded, KMAX + offset, total, 0)
        below = lax.dynamic_slice_in_dim(padded, KMAX - offset, total, 0)
        partial_sum = jnp.where(
            (column_region == index)[None], 1.5 * above + 0.5 * below, partial_sum
        )
    shifted = lax.all_to_all(partial_sum, "egrp", split_axis=0, concat_axis=1, tiled=True).reshape(
        width, rows, cells
    )
    gain_in = lam[None] * dos[:, None, None] * shifted
    new_even = (even + gain_in) / (1.0 + outrate)
    new_odd = odd / (1.0 + outrate + lam[None])
    res = jnp.stack([new_even - even, new_odd - odd])
    res_flat = res.reshape(2, -1)
    cross = jnp.transpose(jnp.sum(flat_g.astype(jnp.float32) * res_flat[None], axis=2))
    self_term = jnp.sum(res_flat * res_flat, axis=1)
    among = lax.dot_general(
        flat_g, flat_g, (((2,), (2,)), ((1,), (1,))), preferred_element_type=jnp.float32
    )
    among, cross, self_term = lax.psum((among, cross, self_term), ("egrp", "space"))
    fields = []
    for field in range(2):
        top = jnp.concatenate([self_term[field][None], cross[field]])[None, :]
        lower_rows = jnp.concatenate([cross[field][:, None], among[field]], axis=1)
        gram = jnp.concatenate([top, lower_rows], axis=0)
        valid = jnp.concatenate([jnp.ones((1,), jnp.float32), hist_used[field].astype(jnp.float32)])
        masked = valid[:, None] * valid[None, :] * gram + jnp.diag(1.0 - valid) * gram[0, 0]
        factor = jnp.linalg.cholesky(masked)
        weights = jax.scipy.linalg.cho_solve((factor, True), valid)
        coeffs = weights / jnp.sum(weights)
        part_mix = coeffs[0] * (dist[field] + 0.5 * res[field])
        for index in range(HISTORY):
            part_mix = part_mix + coeffs[index + 1] * (
                hist_x[index, field].astype(jnp.float32)
                + 0.5 * hist_g[index, field].astype(jnp.float32)
            )
        fields.append(part_mix)
    mixed = jnp.stack(fields)
    mob_block = mobility[None, None]
    wide_field, wide_mob = (
        extended(mixed, (("space", 2),), 1),
        extended(mob_block, (("space", 2),), 1),
    )
    row_ids = lax.axis_index("space") * rows + jnp.arange(rows, dtype=jnp.int32)
    all_rows = lax.axis_size("space") * rows
    cell_ids = jnp.arange(cells, dtype=jnp.int32)
    column_ids = cell_ids % COLS
    lap = jnp.zeros(mixed.shape, jnp.float32)
    lap = add_face(
        lap,
        mixed,
        wide_field[:, :, 0:rows],
        mob_block,
        wide_mob[:, :, 0:rows],
        (row_ids > 0)[:, None],
    )
    lap = add_face(
        lap,
        mixed,
        wide_field[:, :, 2 : rows + 2],
        mob_block,
        wide_mob[:, :, 2 : rows + 2],
        (row_ids < all_rows - 1)[:, None],
    )
    for shift_by, valid_cells in (
        (1, column_ids > 0),
        (-1, column_ids < COLS - 1),
        (COLS, cell_ids >= COLS),
        (-COLS, cell_ids < COLS),
    ):
        moved = jnp.roll(mixed, shift_by, axis=3)
        moved_mob = jnp.roll(mob_block, shift_by, axis=3)
        lap = add_face(lap, mixed, moved, mob_block, moved_mob, valid_cells)
    drive = 0.25 * dos[:, None, None]
    out_even = mixed[0] + 0.08 * lap[0] + drive * mixed[1]
    out_odd = mixed[1] + 0.08 * lap[1] - drive * mixed[0]
    return jnp.stack([out_even, out_odd])


def solution(mesh):
    in_specs = (
        P(None, "egrp", "space", None),
        P(None, None, "egrp", "space", None),
        P(None, None, "egrp", "space", None),
        P("space", None),
        P("space", None),
        P(),
        P(),
        P(),
    )
    out_specs = P(None, "egrp", "space", None)
    return jax.shard_map(local, mesh=mesh, in_specs=in_specs, out_specs=out_specs, check_vma=False)
```

profile of v0, /device:TPU:11, one launch (start us, length us, event | category | flops | bytes accessed | tf_op | source)
XLA Modules:
  0.0 195.8 jit_solution(16239742261708099260)
XLA Ops:
  0.0 1.7 fusion.84
  1.7 1.4 copy.175
  3.1 3.8 %all-to-all-start = ((f32[512,2,256]{0,2,1:T(8,128)}), f32[512,2,256]{0,2,1:T(8,128)S(1)}, u32[]{:S(2)}, u32[]{:S(2)}) async-start(f32[512,2,256]{0,2,1:T(8,128)} %bitcast.6), calls=%async_computation | async-start | bytes 2097152 | tf_op jit(solution)/shard_map/all_to_all | solution.py:52
  6.9 4.0 %collective-permute-start = (f32[1,1,1,128]{3,2,1,0:T(1,128)S(1)}, f32[1,1,1,128]{3,2,1,0:T(1,128)S(1)}, u32[]{:S(2)}, u32[]{:S(2)}) collective-permute-start(f32[1,1,1,128]{3,2,1,0:T(1,128)S(1)} %get-tuple-element.53), channel_id=1, source_target_pairs={{0,1},{1,2},{2,3},{3,4},{4,5},{5,6},{6,7},{7,8},{8,9},{9,10},{10,1... | collective-permute-start | bytes 1544 | tf_op jit(solution)/shard_map/ppermute | solution.py:18
  10.9 1.9 collective-permute-start.2
  12.9 0.7 fusion.90
  23.6 5.1 %reshape.555 = bf16[4,2,262144]{2,1,0:T(2,128)(2,1)} reshape(bf16[4,2,512,4,128]{4,3,2,1,0:T(4,128)(2,1)} %param.13) | data formatting | bytes 8388608 | tf_op jit(solution)/shard_map/reshape | solution.py:34
  28.7 4.1 %fusion.83 = (bf16[1,1,512,4,128]{4,3,2,1,0:T(4,128)(2,1)}, bf16[1,1,512,4,128]{4,3,2,1,0:T(4,128)(2,1)}, bf16[1,1,512,4,128]{4,3,2,1,0:T(4,128)(2,1)}, bf16[1,1...) fusion(bf16[4,2,512,4,128]{4,3,2,1,0:T(4,128)(2,1)} %param.13), kind=kLoop, calls=%fused_computation.196 | loop fusion | bytes 8388608 | tf_op jit(solution)/shard_map/slice | solution.py:97
  33.1 0.7 fusion.89
  33.7 2.5 %add_multiply_fusion.2 = (f32[512]{0:T(512)S(1)}, f32[512]{0:T(512)S(1)}) fusion(s32[]{:T(128)} %bitcast.10, f32[]{:T(128)} %bitcast.2, s32[]{:T(128)S(6)} %mul.605, s32[]{:T(128)} %bitcast.9, f32[]{:T(128)} %bitcast.1), kind=kLoop, calls=%fused_computation.143 | loop fusion | flops 17920 | bytes 4116 | tf_op jit(solution)/shard_map/mul | solution.py:49
  36.2 2.5 %add_multiply_fusion = (f32[512]{0:T(512)S(1)}, f32[512]{0:T(512)S(1)}) fusion(s32[]{:T(128)} %bitcast.12, f32[]{:T(128)} %bitcast.4, s32[]{:T(128)S(6)} %mul.605, s32[]{:T(128)} %bitcast.11, f32[]{:T(128)} %bitcast.3), kind=kLoop, calls=%fused_computation.141 | loop fusion | flops 17920 | bytes 4116 | tf_op jit(solution)/shard_map/mul | solution.py:49
  38.7 2.4 %select_select_fusion.2 = (f32[4,128]{1,0:T(4,128)S(1)}, pred[4,128]{1,0:T(4,128)(4,1)S(1)}, pred[4,128]{1,0:T(4,128)(4,1)S(1)}, pred[4,128]{1,0:T(4,128)(4,1)S(1)}, pred[4,128]{1,0:T(4,128)(4,1)S(1)}) fusion(f32[]{:T(128)} %bitcast.4, f32[]{:T(128)} %bitcast.3, f32[]{:T(128)} %bitcast.2, f32[]{:T(128)} %bitcast.1, s32[4,128]{1,0:T(4,128)S(1)} %copy-done.22), kind=kLoop, calls=%fused_computation.163 | loop fusion | flops 4096 | bytes 6160 | tf_op jit(solution)/shard_map/jit(_where)/select_n | solution.py:51
  41.5 4.1 %fusion.82 = (bf16[1,1,512,4,128]{4,3,2,1,0:T(4,128)(2,1)}, bf16[1,1,512,4,128]{4,3,2,1,0:T(4,128)(2,1)}, bf16[1,1,512,4,128]{4,3,2,1,0:T(4,128)(2,1)}, bf16[1,1...) fusion(bf16[4,2,512,4,128]{4,3,2,1,0:T(4,128)(2,1)} %param.12), kind=kLoop, calls=%fused_computation.195 | loop fusion | bytes 8388608 | tf_op jit(solution)/shard_map/slice | solution.py:96
  45.7 2.2 %copy.185 = bf16[1,1,512,4,128]{2,4,3,1,0:T(8,128)(2,1)} copy(bf16[1,1,512,4,128]{4,3,2,1,0:T(4,128)(2,1)} %get-tuple-element.22) | data formatting | bytes 1048576
  47.9 1.1 copy.186
  49.0 2.1 %copy.187 = bf16[1,1,512,4,128]{2,4,3,1,0:T(8,128)(2,1)} copy(bf16[1,1,512,4,128]{4,3,2,1,0:T(4,128)(2,1)} %get-tuple-element.21) | data formatting | bytes 1048576
  51.1 1.1 copy.188
  52.2 2.2 %copy.189 = bf16[1,1,512,4,128]{2,4,3,1,0:T(8,128)(2,1)} copy(bf16[1,1,512,4,128]{4,3,2,1,0:T(4,128)(2,1)} %get-tuple-element.20) | data formatting | bytes 1048576
  54.4 2.2 %copy.190 = bf16[1,1,512,4,128]{2,4,3,1,0:T(8,128)(2,1)} copy(bf16[1,1,512,4,128]{4,3,2,1,0:T(4,128)(2,1)} %get-tuple-element.28) | data formatting | bytes 1048576
  56.6 2.1 %copy.191 = bf16[1,1,512,4,128]{2,4,3,1,0:T(8,128)(2,1)} copy(bf16[1,1,512,4,128]{4,3,2,1,0:T(4,128)(2,1)} %get-tuple-element.26) | data formatting | bytes 1048576
  58.7 1.2 copy.192
  59.8 2.2 %copy.177 = bf16[1,1,512,4,128]{2,4,3,1,0:T(8,128)(2,1)} copy(bf16[1,1,512,4,128]{4,3,2,1,0:T(4,128)(2,1)} %get-tuple-element.19) | data formatting | bytes 1048576
  62.0 1.2 copy.178
  63.2 1.1 copy.179
  65.0 2.3 %fusion.25 = f32[1024,256]{1,0:T(8,128)} fusion(s32[]{:T(128)S(6)} %select_n.228, f32[1024,256]{1,0:T(8,128)S(1)} %bitcast.141, s32[]{:T(128)S(6)} %select_n.229, s32[]{:T(128)S(6)} %select_n.230, s32[]{:T(128)S(6)} %select_n.231, s32[]{:T(128)S(6)} %select_n.232, s32[]{:T(128)S(6)} %select_n.233, s32[]{:T(128)S(6)} %select_n.234, s32[]{:T(128)S(6)} %select_n.235, ...), kind=kLoop, calls=%fused_computation.64 | loop fusion | flops 4194304 | bytes 2098208 | tf_op jit(solution)/shard_map/jit(_where)/select_n | solution.py:66
  67.3 3.8 %all-to-all-start.1 = ((f32[2,512,256]{2,1,0:T(8,128)}), f32[2,512,256]{2,1,0:T(8,128)S(1)}, u32[]{:S(2)}, u32[]{:S(2)}) async-start(f32[2,512,256]{2,1,0:T(8,128)} %bitcast.13), calls=%async_computation.1 | async-start | bytes 2097152 | tf_op jit(solution)/shard_map/all_to_all | solution.py:69
  71.1 9.5 %fusion = f32[2,4,4]{2,1,0:T(4,128)S(1)} fusion(bf16[4,2,262144]{2,1,0:T(2,128)(2,1)} %reshape.555), kind=kOutput, calls=%fused_computation.18 | convolution fusion | flops 16777216 | bytes 4194432 | tf_op jit(solution)/shard_map/dot_general | solution.py:79
  80.6 2.2 %copy.180 = bf16[1,1,512,4,128]{2,4,3,1,0:T(8,128)(2,1)} copy(bf16[1,1,512,4,128]{4,3,2,1,0:T(4,128)(2,1)} %get-tuple-element.33) | data formatting | bytes 1048576
  82.8 2.1 %copy.181 = bf16[1,1,512,4,128]{2,4,3,1,0:T(8,128)(2,1)} copy(bf16[1,1,512,4,128]{4,3,2,1,0:T(4,128)(2,1)} %get-tuple-element.24) | data formatting | bytes 1048576
  84.9 1.1 copy.182
  86.0 2.1 %copy.183 = bf16[1,1,512,4,128]{2,4,3,1,0:T(8,128)(2,1)} copy(bf16[1,1,512,4,128]{4,3,2,1,0:T(4,128)(2,1)} %get-tuple-element.23) | data formatting | bytes 1048576
  88.1 1.1 copy.184
  89.3 1.3 copy.141
  90.6 2.3 %divide_subtract_fusion.1 = (f32[1,512,4,128]{1,3,2,0:T(8,128)S(1)}, f32[1,512,4,128]{1,3,2,0:T(8,128)S(1)}) fusion(f32[1,512,4,128]{1,3,2,0:T(8,128)} %copy.175, f32[1,512,4,128]{1,3,2,0:T(8,128)} %bitcast.146, f32[512]{0:T(512)S(1)} %get-tuple-element.98, f32[512]{0:T(512)S(1)} %get-tuple-element.99, f32[512]{0:T(512)S(1)} %get-tuple-element.100, ...), kind=kLoop, calls=%fused_computation.94 | loop fusion | flops 3407872 | bytes 5257216 | tf_op jit(solution)/shard_map/sub | solution.py:75
  92.9 1.3 copy.142
  94.2 1.3 copy.144
  95.6 1.6 pad_maximum_fusion.5
  97.2 2.9 %copy.145 = f32[2,512,4,128]{3,2,1,0:T(4,128)} copy(f32[2,512,4,128]{1,3,2,0:T(8,128)} %pad_maximum_fusion.5) | data formatting | bytes 4194304 | tf_op jit(solution)/shard_map/stack | solution.py:75
  100.1 5.3 %multiply_reduce_fusion = f32[4,2]{1,0:T(4,128)S(1)} fusion(bf16[4,2,512,4,128]{4,3,2,1,0:T(4,128)(2,1)} %param.13, f32[2,512,4,128]{3,2,1,0:T(4,128)} %copy.145), kind=kLoop, calls=%fused_computation | loop fusion | flops 6291448 | bytes 6291488 | tf_op jit(solution)/shard_map/reduce_sum | solution.py:77
  105.4 2.3 %fusion.15 = f32[2]{0:T(128)S(1)} fusion(f32[1,262144]{1,0:T(1,128)S(1)} %bitcast.143, f32[1,262144]{1,0:T(1,128)S(1)} %bitcast.142), kind=kLoop, calls=%fused_computation.38 | loop fusion | flops 1572862 | bytes 2097160 | tf_op jit(solution)/shard_map/reduce_sum | solution.py:78
  107.7 40.7 %all-reduce.1 = (f32[2,4,4]{2,1,0:T(4,128)S(1)}, f32[2,4]{0,1:T(4,128)S(1)}, f32[2]{0:T(128)S(1)}) all-reduce(f32[2,4,4]{2,1,0:T(4,128)S(1)} %fusion, f32[2,4]{0,1:T(4,128)S(1)} %bitcast.152, f32[2]{0:T(128)S(1)} %fusion.15), channel_id=1, replica_groups=mesh['egrp'=2,'space'=16] {'egrp','space'}, use_global_device_ids=true, to_apply=%region_4.5 | all-reduce | flops 42 | bytes 336 | tf_op jit(solution)/shard_map/psum | solution.py:82
  148.5 0.6 fusion.87
  149.3 0.7 maximum_bitcast_fusion.1
  150.9 0.7 compare_reduce_fusion
  151.6 0.6 fusion.50
  152.8 0.8 fusion.92
  153.6 0.6 broadcast_divide_fusion
  154.2 0.6 fusion.88
  154.9 0.7 maximum_bitcast_fusion
  156.6 0.6 compare_reduce_fusion.1
  157.2 0.6 fusion.49
  158.5 0.8 fusion.91
  159.2 0.6 broadcast_divide_fusion.1
  159.9 0.7 fusion.86
  160.6 6.4 %bitcast_add_fusion = f32[1,512,4,128]{1,3,2,0:T(8,128)S(1)} fusion(bf16[1,1,512,4,128]{2,4,3,1,0:T(8,128)(2,1)} %copy.192, bf16[1,1,512,4,128]{2,4,3,1,0:T(8,128)(2,1)} %copy.191, bf16[1,1,512,4,128]{2,4,3,1,0:T(8,128)(2,1)} %copy.190, bf16[1,1,512,4,128]{2,4,3,1,0:T(8,128)(2,1)} %copy.189, bf16[1,1,512,4,128]{2,4,3,1,0:T(8,128)(2,1)} %copy.188, ...), kind=kLoop, calls=%fused_computation.86 | loop fusion | flops 9175040 | bytes 6303764 | tf_op jit(solution)/shard_map/add | solution.py:95
  167.1 5.4 %bitcast_add_fusion.4 = f32[1,512,4,128]{1,3,2,0:T(8,128)S(1)} fusion(bf16[1,1,512,4,128]{2,4,3,1,0:T(8,128)(2,1)S(1)} %copy-done.18, bf16[1,1,512,4,128]{2,4,3,1,0:T(8,128)(2,1)S(1)} %copy-done.17, bf16[1,1,512,4,128]{2,4,3,1,0:T(8,128)(2,1)S(1)} %copy-done.16, bf16[1,1,512,4,128]{2,4,3,1,0:T(8,128)(2,1)S(1)} %copy-done.15, ...), kind=kLoop, calls=%fused_computation.90 | loop fusion | flops 7077888 | bytes 7340052 | tf_op jit(solution)/shard_map/add | solution.py:95
  172.5 4.5 %collective-permute-start.1 = (f32[2,512,1,128]{1,3,2,0:T(8,128)S(1)}, f32[2,512,1,128]{1,3,2,0:T(8,128)S(1)}, u32[]{:S(2)}, u32[]{:S(2)}) collective-permute-start(f32[2,512,1,128]{1,3,2,0:T(8,128)S(1)} %get-tuple-element.41), channel_id=1, source_target_pairs={{0,1},{1,2},{2,3},{3,4},{4,5},{5,6},{6,7},{7,8},{8,9},{9,10},{10,1... | collective-permute-start | bytes 1572872 | tf_op jit(solution)/shard_map/ppermute | solution.py:18
  177.0 1.9 collective-permute-start.3
  179.2 0.5 fusion.3
  179.7 9.0 %collective-permute-done.1 = f32[2,512,1,128]{1,3,2,0:T(8,128)S(1)} collective-permute-done((f32[2,512,1,128]{1,3,2,0:T(8,128)S(1)}, f32[2,512,1,128]{1,3,2,0:T(8,128)S(1)}, u32[]{:S(2)}, u32[]{:S(2)}) %collective-permute-start.1) | collective-permute-done | bytes 524320 | tf_op jit(solution)/shard_map/ppermute | solution.py:18
  188.7 1.6 collective-permute-done.3
  190.3 2.9 %fusion.11 = f32[2,512,4,128]{1,3,2,0:T(8,128)S(1)} fusion(f32[2,512,1,128]{1,3,2,0:T(8,128)S(1)} %collective-permute-done.3, f32[1,512,4,128]{1,3,2,0:T(8,128)S(1)} %bitcast_add_fusion, f32[1,512,4,128]{1,3,2,0:T(8,128)S(1)} %bitcast_add_fusion.4, f32[2,512,1,128]{1,3,2,0:T(8,128)S(1)} %collective-permute-done.1, ...), kind=kLoop, calls=%fused_computation.30 | loop fusion | flops 15204352 | bytes 11545096 | tf_op jit(solution)/shard_map/add | solution.py:27
  193.2 0.5 fusion.44
  194.0 1.8 copy.174
  (93 shorter events, 5.2 us)
Async XLA Ops:
  1.7 5.3 %copy-start.19 = (f32[4,128]{1,0:T(4,128)S(1)}, f32[4,128]{1,0:T(4,128)}, u32[]{:S(2)}) copy-start(f32[4,128]{1,0:T(4,128)} %param.14) | copy-start | bytes 6148
  1.7 11.2 %copy-start.20 = (s32[4]{0:T(128)S(1)}, s32[4]{0:T(128)}, u32[]{:S(2)}) copy-start(s32[4]{0:T(128)} %param.16) | copy-start | bytes 52
  3.1 61.6 %all-to-all-start = ((f32[512,2,256]{0,2,1:T(8,128)}), f32[512,2,256]{0,2,1:T(8,128)S(1)}, u32[]{:S(2)}, u32[]{:S(2)}) async-start(f32[512,2,256]{0,2,1:T(8,128)} %bitcast.6), calls=%async_computation | async-start | bytes 2097152 | tf_op jit(solution)/shard_map/all_to_all | solution.py:52
  6.9 82.3 %collective-permute-start = (f32[1,1,1,128]{3,2,1,0:T(1,128)S(1)}, f32[1,1,1,128]{3,2,1,0:T(1,128)S(1)}, u32[]{:S(2)}, u32[]{:S(2)}) collective-permute-start(f32[1,1,1,128]{3,2,1,0:T(1,128)S(1)} %get-tuple-element.53), channel_id=1, source_target_pairs={{0,1},{1,2},{2,3},{3,4},{4,5},{5,6},{6,7},{7,8},{8,9},{9,10},{10,1... | collective-permute-start | bytes 1544 | tf_op jit(solution)/shard_map/ppermute | solution.py:18
  10.9 78.3 %collective-permute-start.2 = (f32[1,1,1,128]{3,2,1,0:T(1,128)S(1)}, f32[1,1,1,128]{3,2,1,0:T(1,128)S(1)}, u32[]{:S(2)}, u32[]{:S(2)}) collective-permute-start(f32[1,1,1,128]{3,2,1,0:T(1,128)S(1)} %get-tuple-element.54), channel_id=1, source_target_pairs={{1,0},{2,1},{3,2},{4,3},{5,4},{6,5},{7,6},{8,7},{9,8},{10,9},{11,1... | collective-permute-start | bytes 1544 | tf_op jit(solution)/shard_map/ppermute | solution.py:21
  28.7 4.3 %copy-start.21 = (f32[4]{0:T(128)S(1)}, f32[4]{0:T(128)}, u32[]{:S(2)}) copy-start(f32[4]{0:T(128)} %param.17) | copy-start | bytes 52
  28.7 10.0 %copy-start.22 = (s32[4,128]{1,0:T(4,128)S(1)}, s32[4,128]{1,0:T(4,128)}, u32[]{:S(2)}) copy-start(s32[4,128]{1,0:T(4,128)} %param.15) | copy-start | bytes 6148
  32.8 8.7 %copy-start.23 = (s32[2,4]{1,0:T(2,128)S(1)}, s32[2,4]{1,0:T(2,128)}, u32[]{:S(2)}) copy-start(s32[2,4]{1,0:T(2,128)} %param.18) | copy-start | bytes 100
  41.5 6.3 %copy-start.7 = (bf16[1,1,512,4,128]{4,3,2,1,0:T(4,128)(2,1)S(1)}, bf16[1,1,512,4,128]{4,3,2,1,0:T(4,128)(2,1)}, u32[]{:S(2)}) copy-start(bf16[1,1,512,4,128]{4,3,2,1,0:T(4,128)(2,1)} %get-tuple-element.30) | copy-start | bytes 1572868
  45.7 5.4 %copy-start.6 = (bf16[1,1,512,4,128]{4,3,2,1,0:T(4,128)(2,1)S(1)}, bf16[1,1,512,4,128]{4,3,2,1,0:T(4,128)(2,1)}, u32[]{:S(2)}) copy-start(bf16[1,1,512,4,128]{4,3,2,1,0:T(4,128)(2,1)} %get-tuple-element.29) | copy-start | bytes 1572868
  51.1 7.6 %copy-start.5 = (bf16[1,1,512,4,128]{4,3,2,1,0:T(4,128)(2,1)S(1)}, bf16[1,1,512,4,128]{4,3,2,1,0:T(4,128)(2,1)}, u32[]{:S(2)}) copy-start(bf16[1,1,512,4,128]{4,3,2,1,0:T(4,128)(2,1)} %get-tuple-element.34) | copy-start | bytes 1572868
  54.4 7.7 %copy-start.4 = (bf16[1,1,512,4,128]{4,3,2,1,0:T(4,128)(2,1)S(1)}, bf16[1,1,512,4,128]{4,3,2,1,0:T(4,128)(2,1)}, u32[]{:S(2)}) copy-start(bf16[1,1,512,4,128]{4,3,2,1,0:T(4,128)(2,1)} %get-tuple-element.27) | copy-start | bytes 1572868
  59.8 3.4 %copy-start.8 = (bf16[1,1,512,4,128]{4,3,2,1,0:T(4,128)(2,1)S(1)}, bf16[1,1,512,4,128]{4,3,2,1,0:T(4,128)(2,1)}, u32[]{:S(2)}) copy-start(bf16[1,1,512,4,128]{4,3,2,1,0:T(4,128)(2,1)} %get-tuple-element.25) | copy-start | bytes 1572868
  67.3 22.0 %all-to-all-start.1 = ((f32[2,512,256]{2,1,0:T(8,128)}), f32[2,512,256]{2,1,0:T(8,128)S(1)}, u32[]{:S(2)}, u32[]{:S(2)}) async-start(f32[2,512,256]{2,1,0:T(8,128)} %bitcast.13), calls=%async_computation.1 | async-start | bytes 2097152 | tf_op jit(solution)/shard_map/all_to_all | solution.py:69
  80.6 4.3 %copy-start.3 = (bf16[1,1,512,4,128]{4,3,2,1,0:T(4,128)(2,1)S(1)}, bf16[1,1,512,4,128]{4,3,2,1,0:T(4,128)(2,1)}, u32[]{:S(2)}) copy-start(bf16[1,1,512,4,128]{4,3,2,1,0:T(4,128)(2,1)} %get-tuple-element.32) | copy-start | bytes 1572868
  80.6 7.5 %copy-start.2 = (bf16[1,1,512,4,128]{4,3,2,1,0:T(4,128)(2,1)S(1)}, bf16[1,1,512,4,128]{4,3,2,1,0:T(4,128)(2,1)}, u32[]{:S(2)}) copy-start(bf16[1,1,512,4,128]{4,3,2,1,0:T(4,128)(2,1)} %get-tuple-element.31) | copy-start | bytes 1572868
  100.1 5.3 %copy-start = (f32[1,512,4,128]{3,2,1,0:T(4,128)S(1)}, f32[1,512,4,128]{3,2,1,0:T(4,128)}, u32[]{:S(2)}) copy-start(f32[1,512,4,128]{3,2,1,0:T(4,128)} %copy.142) | copy-start | bytes 3145732
  100.1 5.3 %copy-start.1 = (f32[1,512,4,128]{3,2,1,0:T(4,128)S(1)}, f32[1,512,4,128]{3,2,1,0:T(4,128)}, u32[]{:S(2)}) copy-start(f32[1,512,4,128]{3,2,1,0:T(4,128)} %copy.144) | copy-start | bytes 3145732
  105.4 55.1 %copy-start.9 = (bf16[1,1,512,4,128]{2,4,3,1,0:T(8,128)(2,1)S(1)}, bf16[1,1,512,4,128]{2,4,3,1,0:T(8,128)(2,1)}, u32[]{:S(2)}) copy-start(bf16[1,1,512,4,128]{2,4,3,1,0:T(8,128)(2,1)} %copy.185) | copy-start | bytes 1572868
  105.4 55.1 %copy-start.11 = (bf16[1,1,512,4,128]{2,4,3,1,0:T(8,128)(2,1)S(1)}, bf16[1,1,512,4,128]{2,4,3,1,0:T(8,128)(2,1)}, u32[]{:S(2)}) copy-start(bf16[1,1,512,4,128]{2,4,3,1,0:T(8,128)(2,1)} %copy.186) | copy-start | bytes 1572868
  160.6 6.4 %copy-start.10 = (bf16[1,1,512,4,128]{2,4,3,1,0:T(8,128)(2,1)S(1)}, bf16[1,1,512,4,128]{2,4,3,1,0:T(8,128)(2,1)}, u32[]{:S(2)}) copy-start(bf16[1,1,512,4,128]{2,4,3,1,0:T(8,128)(2,1)} %copy.177) | copy-start | bytes 1572868
  160.6 6.4 %copy-start.12 = (bf16[1,1,512,4,128]{2,4,3,1,0:T(8,128)(2,1)S(1)}, bf16[1,1,512,4,128]{2,4,3,1,0:T(8,128)(2,1)}, u32[]{:S(2)}) copy-start(bf16[1,1,512,4,128]{2,4,3,1,0:T(8,128)(2,1)} %copy.178) | copy-start | bytes 1572868
  160.6 6.4 %copy-start.13 = (bf16[1,1,512,4,128]{2,4,3,1,0:T(8,128)(2,1)S(1)}, bf16[1,1,512,4,128]{2,4,3,1,0:T(8,128)(2,1)}, u32[]{:S(2)}) copy-start(bf16[1,1,512,4,128]{2,4,3,1,0:T(8,128)(2,1)} %copy.179) | copy-start | bytes 1572868
  160.6 6.4 %copy-start.14 = (bf16[1,1,512,4,128]{2,4,3,1,0:T(8,128)(2,1)S(1)}, bf16[1,1,512,4,128]{2,4,3,1,0:T(8,128)(2,1)}, u32[]{:S(2)}) copy-start(bf16[1,1,512,4,128]{2,4,3,1,0:T(8,128)(2,1)} %copy.180) | copy-start | bytes 1572868
  160.6 6.4 %copy-start.15 = (bf16[1,1,512,4,128]{2,4,3,1,0:T(8,128)(2,1)S(1)}, bf16[1,1,512,4,128]{2,4,3,1,0:T(8,128)(2,1)}, u32[]{:S(2)}) copy-start(bf16[1,1,512,4,128]{2,4,3,1,0:T(8,128)(2,1)} %copy.181) | copy-start | bytes 1572868
  160.6 6.4 %copy-start.16 = (bf16[1,1,512,4,128]{2,4,3,1,0:T(8,128)(2,1)S(1)}, bf16[1,1,512,4,128]{2,4,3,1,0:T(8,128)(2,1)}, u32[]{:S(2)}) copy-start(bf16[1,1,512,4,128]{2,4,3,1,0:T(8,128)(2,1)} %copy.182) | copy-start | bytes 1572868
  160.6 6.4 %copy-start.17 = (bf16[1,1,512,4,128]{2,4,3,1,0:T(8,128)(2,1)S(1)}, bf16[1,1,512,4,128]{2,4,3,1,0:T(8,128)(2,1)}, u32[]{:S(2)}) copy-start(bf16[1,1,512,4,128]{2,4,3,1,0:T(8,128)(2,1)} %copy.183) | copy-start | bytes 1572868
  160.6 6.4 %copy-start.18 = (bf16[1,1,512,4,128]{2,4,3,1,0:T(8,128)(2,1)S(1)}, bf16[1,1,512,4,128]{2,4,3,1,0:T(8,128)(2,1)}, u32[]{:S(2)}) copy-start(bf16[1,1,512,4,128]{2,4,3,1,0:T(8,128)(2,1)} %copy.184) | copy-start | bytes 1572868
  172.5 16.2 %collective-permute-start.1 = (f32[2,512,1,128]{1,3,2,0:T(8,128)S(1)}, f32[2,512,1,128]{1,3,2,0:T(8,128)S(1)}, u32[]{:S(2)}, u32[]{:S(2)}) collective-permute-start(f32[2,512,1,128]{1,3,2,0:T(8,128)S(1)} %get-tuple-element.41), channel_id=1, source_target_pairs={{0,1},{1,2},{2,3},{3,4},{4,5},{5,6},{6,7},{7,8},{8,9},{9,10},{10,1... | collective-permute-start | bytes 1572872 | tf_op jit(solution)/shard_map/ppermute | solution.py:18
  177.0 13.3 %collective-permute-start.3 = (f32[2,512,1,128]{1,3,2,0:T(8,128)S(1)}, f32[2,512,1,128]{1,3,2,0:T(8,128)S(1)}, u32[]{:S(2)}, u32[]{:S(2)}) collective-permute-start(f32[2,512,1,128]{1,3,2,0:T(8,128)S(1)} %get-tuple-element.42), channel_id=1, source_target_pairs={{1,0},{2,1},{3,2},{4,3},{5,4},{6,5},{7,6},{8,7},{9,8},{10,9},{11,1... | collective-permute-start | bytes 1572872 | tf_op jit(solution)/shard_map/ppermute | solution.py:21
where the time goes:
time: 197 us; the launch traced here: 196 us
  local copies, waits for them, and re-layouts  57.4 us (29%)
  other arithmetic  45.2 us (23%)
  blocking collectives  40.7 us (21%)
  starting transfers between devices  19.9 us (10%)
  matrix products  11.5 us (6%)
  waiting for transfers between devices  10.6 us (5%)
  between operations  10.6 us (5%)
    psum x1, blocking collectives, local(): lax.psum((among, cross, self_term), ('egrp', 'space'))  40.7 us
    unnamed x66, local copies, waits for them, and re-layouts  29.2 us
    add x2, other arithmetic, local(): part_mix + coeffs[index + 1] * (hist_x[index, field].astype(jnp.float32)...  11.7 us
    dot_general x1, matrix products, local(): lax.dot_general(flat_g, flat_g, (((2,), (2,)), ((1,), (1,))), preferred_e...  9.54 us
    ppermute x2, waiting for transfers between devices, extended(): lax.ppermute(lax.slice_in_dim(block, block.shape[dim] - width, None, axis...  9 us
    ppermute x2, starting transfers between devices, extended(): lax.ppermute(lax.slice_in_dim(block, block.shape[dim] - width, None, axis...  8.46 us
    reduce_sum x1, other arithmetic, local(): jnp.sum(flat_g.astype(jnp.float32) * res_flat[None], axis=2)  5.32 us
    reshape x1, local copies, waits for them, and re-layouts, local(): flat_g = hist_g.reshape(HISTORY, 2, -1)  5.11 us
  transfers between devices with their start and end apart: 6, of which 2 were waited for; matrix products, arithmetic and copies ran while one was open for 32% of the time, Pallas kernels for 0%

commit v1 on v0

--- a/solution.py
+++ b/solution.py
@@ -8,6 +8,11 @@
 NREGION = 4
 KMAX = 64
 COLS = 64
+
+
+def axis_by_axis(x, axis_one, axis_two):
+    partial = lax.psum(x, axis_one)
+    return lax.psum(partial, axis_two)
 
 
 def extended(block, sides, width):
@@ -79,7 +84,7 @@
     among = lax.dot_general(
         flat_g, flat_g, (((2,), (2,)), ((1,), (1,))), preferred_element_type=jnp.float32
     )
-    among, cross, self_term = lax.psum((among, cross, self_term), ("egrp", "space"))
+    among, cross, self_term = axis_by_axis((among, cross, self_term), "space", "egrp")
     fields = []
     for field in range(2):
         top = jnp.concatenate([self_term[field][None], cross[field]])[None, :]

time: 197 us -> 187 us (0.949)
  the two profiles are of different devices: /device:TPU:11 before, /device:TPU:6 now
where the time goes in v1:
time: 187 us; the launch traced here: 186 us
  local copies, waits for them, and re-layouts  57.4 us (31%)
  other arithmetic  45.1 us (24%)
  blocking collectives  33.4 us (18%)
  starting transfers between devices  19 us (10%)
  matrix products  11.4 us (6%)
  between operations  10.1 us (5%)
  waiting for transfers between devices  9.76 us (5%)
    unnamed x66, local copies, waits for them, and re-layouts  29.2 us
    psum x1, blocking collectives, axis_by_axis(): partial = lax.psum(x, axis_one)  28.4 us
    add x2, other arithmetic, local(): part_mix + coeffs[index + 1] * (hist_x[index, field].astype(jnp.float32)...  11.7 us
    ppermute x2, waiting for transfers between devices, extended(): lax.ppermute(lax.slice_in_dim(block, block.shape[dim] - width, None, axis...  9.75 us
    dot_general x1, matrix products, local(): lax.dot_general(flat_g, flat_g, (((2,), (2,)), ((1,), (1,))), preferred_e...  9.54 us
    ppermute x2, starting transfers between devices, extended(): lax.ppermute(lax.slice_in_dim(block, 0, width, axis=dim), axis, backward)  7.28 us
    reduce_sum x1, other arithmetic, local(): jnp.sum(flat_g.astype(jnp.float32) * res_flat[None], axis=2)  5.32 us
    reshape x1, local copies, waits for them, and re-layouts, local(): flat_g = hist_g.reshape(HISTORY, 2, -1)  5.1 us
  transfers between devices with their start and end apart: 6, of which 1 were waited for; matrix products, arithmetic and copies ran while one was open for 34% of the time, Pallas kernels for 0%

profile of v1, /device:TPU:6, one launch (start us, length us, event | category | flops | bytes accessed | tf_op | source)
XLA Modules:
  0.0 186.2 jit_solution(14561547262903860062)
XLA Ops:
  0.0 1.7 fusion.84
  1.7 1.4 copy.175
  3.1 4.1 %all-to-all-start = ((f32[512,2,256]{0,2,1:T(8,128)}), f32[512,2,256]{0,2,1:T(8,128)S(1)}, u32[]{:S(2)}, u32[]{:S(2)}) async-start(f32[512,2,256]{0,2,1:T(8,128)} %bitcast.6), calls=%async_computation | async-start | bytes 2097152 | tf_op jit(solution)/shard_map/all_to_all | solution.py:57
  7.2 1.9 %collective-permute-start = (f32[1,1,1,128]{3,2,1,0:T(1,128)S(1)}, f32[1,1,1,128]{3,2,1,0:T(1,128)S(1)}, u32[]{:S(2)}, u32[]{:S(2)}) collective-permute-start(f32[1,1,1,128]{3,2,1,0:T(1,128)S(1)} %get-tuple-element.56), channel_id=1, source_target_pairs={{0,1},{1,2},{2,3},{3,4},{4,5},{5,6},{6,7},{7,8},{8,9},{9,10},{10,1... | collective-permute-start | bytes 1544 | tf_op jit(solution)/shard_map/ppermute | solution.py:23
  9.1 3.6 %collective-permute-start.2 = (f32[1,1,1,128]{3,2,1,0:T(1,128)S(1)}, f32[1,1,1,128]{3,2,1,0:T(1,128)S(1)}, u32[]{:S(2)}, u32[]{:S(2)}) collective-permute-start(f32[1,1,1,128]{3,2,1,0:T(1,128)S(1)} %get-tuple-element.57), channel_id=1, source_target_pairs={{1,0},{2,1},{3,2},{4,3},{5,4},{6,5},{7,6},{8,7},{9,8},{10,9},{11,1... | collective-permute-start | bytes 1544 | tf_op jit(solution)/shard_map/ppermute | solution.py:26
  12.8 0.7 fusion.90
  22.9 5.1 %reshape.555 = bf16[4,2,262144]{2,1,0:T(2,128)(2,1)} reshape(bf16[4,2,512,4,128]{4,3,2,1,0:T(4,128)(2,1)} %param.13) | data formatting | bytes 8388608 | tf_op jit(solution)/shard_map/reshape | solution.py:39
  28.0 4.1 %fusion.83 = (bf16[1,1,512,4,128]{4,3,2,1,0:T(4,128)(2,1)}, bf16[1,1,512,4,128]{4,3,2,1,0:T(4,128)(2,1)}, bf16[1,1,512,4,128]{4,3,2,1,0:T(4,128)(2,1)}, bf16[1,1...) fusion(bf16[4,2,512,4,128]{4,3,2,1,0:T(4,128)(2,1)} %param.13), kind=kLoop, calls=%fused_computation.196 | loop fusion | bytes 8388608 | tf_op jit(solution)/shard_map/slice | solution.py:102
  32.4 0.7 fusion.89
  33.1 2.5 %add_multiply_fusion = (f32[512]{0:T(512)S(1)}, f32[512]{0:T(512)S(1)}) fusion(s32[]{:T(128)} %bitcast.12, f32[]{:T(128)} %bitcast.4, s32[]{:T(128)S(6)} %mul.605, s32[]{:T(128)} %bitcast.11, f32[]{:T(128)} %bitcast.3), kind=kLoop, calls=%fused_computation.141 | loop fusion | flops 17920 | bytes 4116 | tf_op jit(solution)/shard_map/mul | solution.py:54
  35.6 2.5 %add_multiply_fusion.2 = (f32[512]{0:T(512)S(1)}, f32[512]{0:T(512)S(1)}) fusion(s32[]{:T(128)} %bitcast.10, f32[]{:T(128)} %bitcast.2, s32[]{:T(128)S(6)} %mul.605, s32[]{:T(128)} %bitcast.9, f32[]{:T(128)} %bitcast.1), kind=kLoop, calls=%fused_computation.143 | loop fusion | flops 17920 | bytes 4116 | tf_op jit(solution)/shard_map/mul | solution.py:54
  38.1 2.6 %select_select_fusion.2 = (f32[4,128]{1,0:T(4,128)S(1)}, pred[4,128]{1,0:T(4,128)(4,1)S(1)}, pred[4,128]{1,0:T(4,128)(4,1)S(1)}, pred[4,128]{1,0:T(4,128)(4,1)S(1)}, pred[4,128]{1,0:T(4,128)(4,1)S(1)}) fusion(f32[]{:T(128)} %bitcast.4, f32[]{:T(128)} %bitcast.3, f32[]{:T(128)} %bitcast.2, f32[]{:T(128)} %bitcast.1, s32[4,128]{1,0:T(4,128)S(1)} %copy-done.22), kind=kLoop, calls=%fused_computation.163 | loop fusion | flops 4096 | bytes 6160 | tf_op jit(solution)/shard_map/jit(_where)/select_n | solution.py:56
  41.1 4.1 %fusion.82 = (bf16[1,1,512,4,128]{4,3,2,1,0:T(4,128)(2,1)}, bf16[1,1,512,4,128]{4,3,2,1,0:T(4,128)(2,1)}, bf16[1,1,512,4,128]{4,3,2,1,0:T(4,128)(2,1)}, bf16[1,1...) fusion(bf16[4,2,512,4,128]{4,3,2,1,0:T(4,128)(2,1)} %param.12), kind=kLoop, calls=%fused_computation.195 | loop fusion | bytes 8388608 | tf_op jit(solution)/shard_map/slice | solution.py:101
  45.2 2.2 %copy.185 = bf16[1,1,512,4,128]{2,4,3,1,0:T(8,128)(2,1)} copy(bf16[1,1,512,4,128]{4,3,2,1,0:T(4,128)(2,1)} %get-tuple-element.25) | data formatting | bytes 1048576
  47.4 1.1 copy.186
  48.5 2.1 %copy.187 = bf16[1,1,512,4,128]{2,4,3,1,0:T(8,128)(2,1)} copy(bf16[1,1,512,4,128]{4,3,2,1,0:T(4,128)(2,1)} %get-tuple-element.24) | data formatting | bytes 1048576
  50.6 1.1 copy.188
  51.8 2.2 %copy.189 = bf16[1,1,512,4,128]{2,4,3,1,0:T(8,128)(2,1)} copy(bf16[1,1,512,4,128]{4,3,2,1,0:T(4,128)(2,1)} %get-tuple-element.23) | data formatting | bytes 1048576
  53.9 2.2 %copy.190 = bf16[1,1,512,4,128]{2,4,3,1,0:T(8,128)(2,1)} copy(bf16[1,1,512,4,128]{4,3,2,1,0:T(4,128)(2,1)} %get-tuple-element.31) | data formatting | bytes 1048576
  56.1 2.1 %copy.191 = bf16[1,1,512,4,128]{2,4,3,1,0:T(8,128)(2,1)} copy(bf16[1,1,512,4,128]{4,3,2,1,0:T(4,128)(2,1)} %get-tuple-element.29) | data formatting | bytes 1048576
  58.3 1.2 copy.192
  59.4 2.2 %copy.177 = bf16[1,1,512,4,128]{2,4,3,1,0:T(8,128)(2,1)} copy(bf16[1,1,512,4,128]{4,3,2,1,0:T(4,128)(2,1)} %get-tuple-element.22) | data formatting | bytes 1048576
  61.6 1.2 copy.178
  62.8 1.1 copy.179
  64.6 2.3 %fusion.25 = f32[1024,256]{1,0:T(8,128)} fusion(s32[]{:T(128)S(6)} %select_n.228, f32[1024,256]{1,0:T(8,128)S(1)} %bitcast.141, s32[]{:T(128)S(6)} %select_n.229, s32[]{:T(128)S(6)} %select_n.230, s32[]{:T(128)S(6)} %select_n.231, s32[]{:T(128)S(6)} %select_n.232, s32[]{:T(128)S(6)} %select_n.233, s32[]{:T(128)S(6)} %select_n.234, s32[]{:T(128)S(6)} %select_n.235, ...), kind=kLoop, calls=%fused_computation.64 | loop fusion | flops 4194304 | bytes 2098208 | tf_op jit(solution)/shard_map/jit(_where)/select_n | solution.py:71
  66.9 3.8 %all-to-all-start.1 = ((f32[2,512,256]{2,1,0:T(8,128)}), f32[2,512,256]{2,1,0:T(8,128)S(1)}, u32[]{:S(2)}, u32[]{:S(2)}) async-start(f32[2,512,256]{2,1,0:T(8,128)} %bitcast.13), calls=%async_computation.1 | async-start | bytes 2097152 | tf_op jit(solution)/shard_map/all_to_all | solution.py:74
  70.6 9.5 %fusion = f32[2,4,4]{2,1,0:T(4,128)S(1)} fusion(bf16[4,2,262144]{2,1,0:T(2,128)(2,1)} %reshape.555), kind=kOutput, calls=%fused_computation.18 | convolution fusion | flops 16777216 | bytes 4194432 | tf_op jit(solution)/shard_map/dot_general | solution.py:84
  80.2 2.2 %copy.180 = bf16[1,1,512,4,128]{2,4,3,1,0:T(8,128)(2,1)} copy(bf16[1,1,512,4,128]{4,3,2,1,0:T(4,128)(2,1)} %get-tuple-element.36) | data formatting | bytes 1048576
  82.4 2.1 %copy.181 = bf16[1,1,512,4,128]{2,4,3,1,0:T(8,128)(2,1)} copy(bf16[1,1,512,4,128]{4,3,2,1,0:T(4,128)(2,1)} %get-tuple-element.27) | data formatting | bytes 1048576
  84.5 1.1 copy.182
  85.6 2.1 %copy.183 = bf16[1,1,512,4,128]{2,4,3,1,0:T(8,128)(2,1)} copy(bf16[1,1,512,4,128]{4,3,2,1,0:T(4,128)(2,1)} %get-tuple-element.26) | data formatting | bytes 1048576
  87.7 1.1 copy.184
  88.9 1.3 copy.141
  90.2 2.3 %divide_subtract_fusion.1 = (f32[1,512,4,128]{1,3,2,0:T(8,128)S(1)}, f32[1,512,4,128]{1,3,2,0:T(8,128)S(1)}) fusion(f32[1,512,4,128]{1,3,2,0:T(8,128)} %copy.175, f32[1,512,4,128]{1,3,2,0:T(8,128)} %bitcast.146, f32[512]{0:T(512)S(1)} %get-tuple-element.101, f32[512]{0:T(512)S(1)} %get-tuple-element.102, f32[512]{0:T(512)S(1)} %get-tuple-element.103, ...), kind=kLoop, calls=%fused_computation.94 | loop fusion | flops 3407872 | bytes 5257216 | tf_op jit(solution)/shard_map/sub | solution.py:80
  92.5 1.3 copy.142
  93.8 1.3 copy.144
  95.1 1.6 pad_maximum_fusion.5
  96.7 2.9 %copy.145 = f32[2,512,4,128]{3,2,1,0:T(4,128)} copy(f32[2,512,4,128]{1,3,2,0:T(8,128)} %pad_maximum_fusion.5) | data formatting | bytes 4194304 | tf_op jit(solution)/shard_map/stack | solution.py:80
  99.7 5.3 %multiply_reduce_fusion = f32[4,2]{1,0:T(4,128)S(1)} fusion(bf16[4,2,512,4,128]{4,3,2,1,0:T(4,128)(2,1)} %param.13, f32[2,512,4,128]{3,2,1,0:T(4,128)} %copy.145), kind=kLoop, calls=%fused_computation | loop fusion | flops 6291448 | bytes 6291488 | tf_op jit(solution)/shard_map/reduce_sum | solution.py:82
  105.0 2.3 %fusion.15 = f32[2]{0:T(128)S(1)} fusion(f32[1,262144]{1,0:T(1,128)S(1)} %bitcast.143, f32[1,262144]{1,0:T(1,128)S(1)} %bitcast.142), kind=kLoop, calls=%fused_computation.38 | loop fusion | flops 1572862 | bytes 2097160 | tf_op jit(solution)/shard_map/reduce_sum | solution.py:83
  107.3 28.4 %all-reduce.1 = (f32[2,4,4]{2,1,0:T(4,128)S(1)}, f32[2,4]{0,1:T(4,128)S(1)}, f32[2]{0:T(128)S(1)}) all-reduce(f32[2,4,4]{2,1,0:T(4,128)S(1)} %fusion, f32[2,4]{0,1:T(4,128)S(1)} %bitcast.152, f32[2]{0:T(128)S(1)} %fusion.15), channel_id=1, replica_groups=mesh['egrp'=2,'space'=16] {'space'}, use_global_device_ids=true, to_apply=%region_6.7 | all-reduce | flops 42 | bytes 336 | tf_op jit(solution)/shard_map/psum | solution.py:14
  135.7 5.0 %all-reduce.2 = (f32[2,4,4]{2,1,0:T(4,128)S(1)}, f32[2,4]{0,1:T(4,128)S(1)}, f32[2]{0:T(128)S(1)}) all-reduce(f32[2,4,4]{2,1,0:T(4,128)S(1)} %get-tuple-element.9, f32[2,4]{0,1:T(4,128)S(1)} %get-tuple-element.10, f32[2]{0:T(128)S(1)} %get-tuple-element.11), channel_id=1, replica_groups=mesh['egrp'=2,'space'=16] {'egrp'}, use_global_device_ids=true, to_apply=%region_7.8 | all-reduce | flops 42 | bytes 336 | tf_op jit(solution)/shard_map/psum | solution.py:15
  140.9 0.6 fusion.87
  141.5 0.6 maximum_bitcast_fusion.1
  143.2 0.6 compare_reduce_fusion
  143.8 0.6 fusion.50
  145.0 0.7 fusion.92
  145.7 0.6 broadcast_divide_fusion
  146.3 0.7 fusion.88
  146.9 0.7 maximum_bitcast_fusion
  148.6 0.6 compare_reduce_fusion.1
  149.3 0.6 fusion.49
  150.5 0.8 fusion.91
  151.3 0.6 broadcast_divide_fusion.1
  152.0 0.7 fusion.86
  152.7 6.4 %bitcast_add_fusion = f32[1,512,4,128]{1,3,2,0:T(8,128)S(1)} fusion(bf16[1,1,512,4,128]{2,4,3,1,0:T(8,128)(2,1)} %copy.192, bf16[1,1,512,4,128]{2,4,3,1,0:T(8,128)(2,1)} %copy.191, bf16[1,1,512,4,128]{2,4,3,1,0:T(8,128)(2,1)} %copy.190, bf16[1,1,512,4,128]{2,4,3,1,0:T(8,128)(2,1)} %copy.189, bf16[1,1,512,4,128]{2,4,3,1,0:T(8,128)(2,1)} %copy.188, ...), kind=kLoop, calls=%fused_computation.86 | loop fusion | flops 9175040 | bytes 6303764 | tf_op jit(solution)/shard_map/add | solution.py:100
  159.2 5.2 %bitcast_add_fusion.4 = f32[1,512,4,128]{1,3,2,0:T(8,128)S(1)} fusion(bf16[1,1,512,4,128]{2,4,3,1,0:T(8,128)(2,1)S(1)} %copy-done.18, bf16[1,1,512,4,128]{2,4,3,1,0:T(8,128)(2,1)S(1)} %copy-done.17, bf16[1,1,512,4,128]{2,4,3,1,0:T(8,128)(2,1)S(1)} %copy-done.16, bf16[1,1,512,4,128]{2,4,3,1,0:T(8,128)(2,1)S(1)} %copy-done.15, ...), kind=kLoop, calls=%fused_computation.90 | loop fusion | flops 7077888 | bytes 7340052 | tf_op jit(solution)/shard_map/add | solution.py:100
  164.5 1.9 %collective-permute-start.1 = (f32[2,512,1,128]{1,3,2,0:T(8,128)S(1)}, f32[2,512,1,128]{1,3,2,0:T(8,128)S(1)}, u32[]{:S(2)}, u32[]{:S(2)}) collective-permute-start(f32[2,512,1,128]{1,3,2,0:T(8,128)S(1)} %get-tuple-element.44), channel_id=1, source_target_pairs={{0,1},{1,2},{2,3},{3,4},{4,5},{5,6},{6,7},{7,8},{8,9},{9,10},{10,1... | collective-permute-start | bytes 1572872 | tf_op jit(solution)/shard_map/ppermute | solution.py:23
  166.4 3.6 %collective-permute-start.3 = (f32[2,512,1,128]{1,3,2,0:T(8,128)S(1)}, f32[2,512,1,128]{1,3,2,0:T(8,128)S(1)}, u32[]{:S(2)}, u32[]{:S(2)}) collective-permute-start(f32[2,512,1,128]{1,3,2,0:T(8,128)S(1)} %get-tuple-element.45), channel_id=1, source_target_pairs={{1,0},{2,1},{3,2},{4,3},{5,4},{6,5},{7,6},{8,7},{9,8},{10,9},{11,1... | collective-permute-start | bytes 1572872 | tf_op jit(solution)/shard_map/ppermute | solution.py:26
  170.4 0.5 fusion.3
  170.9 9.7 %collective-permute-done.1 = f32[2,512,1,128]{1,3,2,0:T(8,128)S(1)} collective-permute-done((f32[2,512,1,128]{1,3,2,0:T(8,128)S(1)}, f32[2,512,1,128]{1,3,2,0:T(8,128)S(1)}, u32[]{:S(2)}, u32[]{:S(2)}) %collective-permute-start.1) | collective-permute-done | bytes 524320 | tf_op jit(solution)/shard_map/ppermute | solution.py:23
  180.6 2.9 %fusion.11 = f32[2,512,4,128]{1,3,2,0:T(8,128)S(1)} fusion(f32[2,512,1,128]{1,3,2,0:T(8,128)S(1)} %collective-permute-done.3, f32[1,512,4,128]{1,3,2,0:T(8,128)S(1)} %bitcast_add_fusion, f32[1,512,4,128]{1,3,2,0:T(8,128)S(1)} %bitcast_add_fusion.4, f32[2,512,1,128]{1,3,2,0:T(8,128)S(1)} %collective-permute-done.1, ...), kind=kLoop, calls=%fused_computation.30 | loop fusion | flops 15204352 | bytes 11545096 | tf_op jit(solution)/shard_map/add | solution.py:32
  183.5 0.5 fusion.44
  184.4 1.8 copy.174
  (94 shorter events, 5.3 us)
Async XLA Ops:
  1.7 5.5 %copy-start.19 = (f32[4,128]{1,0:T(4,128)S(1)}, f32[4,128]{1,0:T(4,128)}, u32[]{:S(2)}) copy-start(f32[4,128]{1,0:T(4,128)} %param.14) | copy-start | bytes 6148
  1.7 11.1 %copy-start.20 = (s32[4]{0:T(128)S(1)}, s32[4]{0:T(128)}, u32[]{:S(2)}) copy-start(s32[4]{0:T(128)} %param.16) | copy-start | bytes 52
  3.1 61.2 %all-to-all-start = ((f32[512,2,256]{0,2,1:T(8,128)}), f32[512,2,256]{0,2,1:T(8,128)S(1)}, u32[]{:S(2)}, u32[]{:S(2)}) async-start(f32[512,2,256]{0,2,1:T(8,128)} %bitcast.6), calls=%async_computation | async-start | bytes 2097152 | tf_op jit(solution)/shard_map/all_to_all | solution.py:57
  7.2 81.7 %collective-permute-start = (f32[1,1,1,128]{3,2,1,0:T(1,128)S(1)}, f32[1,1,1,128]{3,2,1,0:T(1,128)S(1)}, u32[]{:S(2)}, u32[]{:S(2)}) collective-permute-start(f32[1,1,1,128]{3,2,1,0:T(1,128)S(1)} %get-tuple-element.56), channel_id=1, source_target_pairs={{0,1},{1,2},{2,3},{3,4},{4,5},{5,6},{6,7},{7,8},{8,9},{9,10},{10,1... | collective-permute-start | bytes 1544 | tf_op jit(solution)/shard_map/ppermute | solution.py:23
  9.1 79.7 %collective-permute-start.2 = (f32[1,1,1,128]{3,2,1,0:T(1,128)S(1)}, f32[1,1,1,128]{3,2,1,0:T(1,128)S(1)}, u32[]{:S(2)}, u32[]{:S(2)}) collective-permute-start(f32[1,1,1,128]{3,2,1,0:T(1,128)S(1)} %get-tuple-element.57), channel_id=1, source_target_pairs={{1,0},{2,1},{3,2},{4,3},{5,4},{6,5},{7,6},{8,7},{9,8},{10,9},{11,1... | collective-permute-start | bytes 1544 | tf_op jit(solution)/shard_map/ppermute | solution.py:26
  28.0 4.4 %copy-start.21 = (f32[4]{0:T(128)S(1)}, f32[4]{0:T(128)}, u32[]{:S(2)}) copy-start(f32[4]{0:T(128)} %param.17) | copy-start | bytes 52
  28.0 10.0 %copy-start.22 = (s32[4,128]{1,0:T(4,128)S(1)}, s32[4,128]{1,0:T(4,128)}, u32[]{:S(2)}) copy-start(s32[4,128]{1,0:T(4,128)} %param.15) | copy-start | bytes 6148
  32.1 8.9 %copy-start.23 = (s32[2,4]{1,0:T(2,128)S(1)}, s32[2,4]{1,0:T(2,128)}, u32[]{:S(2)}) copy-start(s32[2,4]{1,0:T(2,128)} %param.18) | copy-start | bytes 100
  41.1 6.3 %copy-start.7 = (bf16[1,1,512,4,128]{4,3,2,1,0:T(4,128)(2,1)S(1)}, bf16[1,1,512,4,128]{4,3,2,1,0:T(4,128)(2,1)}, u32[]{:S(2)}) copy-start(bf16[1,1,512,4,128]{4,3,2,1,0:T(4,128)(2,1)} %get-tuple-element.33) | copy-start | bytes 1572868
  45.2 5.4 %copy-start.6 = (bf16[1,1,512,4,128]{4,3,2,1,0:T(4,128)(2,1)S(1)}, bf16[1,1,512,4,128]{4,3,2,1,0:T(4,128)(2,1)}, u32[]{:S(2)}) copy-start(bf16[1,1,512,4,128]{4,3,2,1,0:T(4,128)(2,1)} %get-tuple-element.32) | copy-start | bytes 1572868
  50.6 7.6 %copy-start.5 = (bf16[1,1,512,4,128]{4,3,2,1,0:T(4,128)(2,1)S(1)}, bf16[1,1,512,4,128]{4,3,2,1,0:T(4,128)(2,1)}, u32[]{:S(2)}) copy-start(bf16[1,1,512,4,128]{4,3,2,1,0:T(4,128)(2,1)} %get-tuple-element.37) | copy-start | bytes 1572868
  53.9 7.7 %copy-start.4 = (bf16[1,1,512,4,128]{4,3,2,1,0:T(4,128)(2,1)S(1)}, bf16[1,1,512,4,128]{4,3,2,1,0:T(4,128)(2,1)}, u32[]{:S(2)}) copy-start(bf16[1,1,512,4,128]{4,3,2,1,0:T(4,128)(2,1)} %get-tuple-element.30) | copy-start | bytes 1572868
  59.4 3.4 %copy-start.8 = (bf16[1,1,512,4,128]{4,3,2,1,0:T(4,128)(2,1)S(1)}, bf16[1,1,512,4,128]{4,3,2,1,0:T(4,128)(2,1)}, u32[]{:S(2)}) copy-start(bf16[1,1,512,4,128]{4,3,2,1,0:T(4,128)(2,1)} %get-tuple-element.28) | copy-start | bytes 1572868
  66.9 22.0 %all-to-all-start.1 = ((f32[2,512,256]{2,1,0:T(8,128)}), f32[2,512,256]{2,1,0:T(8,128)S(1)}, u32[]{:S(2)}, u32[]{:S(2)}) async-start(f32[2,512,256]{2,1,0:T(8,128)} %bitcast.13), calls=%async_computation.1 | async-start | bytes 2097152 | tf_op jit(solution)/shard_map/all_to_all | solution.py:74
  80.2 4.4 %copy-start.3 = (bf16[1,1,512,4,128]{4,3,2,1,0:T(4,128)(2,1)S(1)}, bf16[1,1,512,4,128]{4,3,2,1,0:T(4,128)(2,1)}, u32[]{:S(2)}) copy-start(bf16[1,1,512,4,128]{4,3,2,1,0:T(4,128)(2,1)} %get-tuple-element.35) | copy-start | bytes 1572868
  80.2 7.6 %copy-start.2 = (bf16[1,1,512,4,128]{4,3,2,1,0:T(4,128)(2,1)S(1)}, bf16[1,1,512,4,128]{4,3,2,1,0:T(4,128)(2,1)}, u32[]{:S(2)}) copy-start(bf16[1,1,512,4,128]{4,3,2,1,0:T(4,128)(2,1)} %get-tuple-element.34) | copy-start | bytes 1572868
  99.7 5.3 %copy-start = (f32[1,512,4,128]{3,2,1,0:T(4,128)S(1)}, f32[1,512,4,128]{3,2,1,0:T(4,128)}, u32[]{:S(2)}) copy-start(f32[1,512,4,128]{3,2,1,0:T(4,128)} %copy.142) | copy-start | bytes 3145732
  99.7 5.3 %copy-start.1 = (f32[1,512,4,128]{3,2,1,0:T(4,128)S(1)}, f32[1,512,4,128]{3,2,1,0:T(4,128)}, u32[]{:S(2)}) copy-start(f32[1,512,4,128]{3,2,1,0:T(4,128)} %copy.144) | copy-start | bytes 3145732
  105.0 47.6 %copy-start.9 = (bf16[1,1,512,4,128]{2,4,3,1,0:T(8,128)(2,1)S(1)}, bf16[1,1,512,4,128]{2,4,3,1,0:T(8,128)(2,1)}, u32[]{:S(2)}) copy-start(bf16[1,1,512,4,128]{2,4,3,1,0:T(8,128)(2,1)} %copy.185) | copy-start | bytes 1572868
  105.0 47.6 %copy-start.11 = (bf16[1,1,512,4,128]{2,4,3,1,0:T(8,128)(2,1)S(1)}, bf16[1,1,512,4,128]{2,4,3,1,0:T(8,128)(2,1)}, u32[]{:S(2)}) copy-start(bf16[1,1,512,4,128]{2,4,3,1,0:T(8,128)(2,1)} %copy.186) | copy-start | bytes 1572868
  152.6 6.5 %copy-start.10 = (bf16[1,1,512,4,128]{2,4,3,1,0:T(8,128)(2,1)S(1)}, bf16[1,1,512,4,128]{2,4,3,1,0:T(8,128)(2,1)}, u32[]{:S(2)}) copy-start(bf16[1,1,512,4,128]{2,4,3,1,0:T(8,128)(2,1)} %copy.177) | copy-start | bytes 1572868
  152.6 6.5 %copy-start.12 = (bf16[1,1,512,4,128]{2,4,3,1,0:T(8,128)(2,1)S(1)}, bf16[1,1,512,4,128]{2,4,3,1,0:T(8,128)(2,1)}, u32[]{:S(2)}) copy-start(bf16[1,1,512,4,128]{2,4,3,1,0:T(8,128)(2,1)} %copy.178) | copy-start | bytes 1572868
  152.6 6.5 %copy-start.13 = (bf16[1,1,512,4,128]{2,4,3,1,0:T(8,128)(2,1)S(1)}, bf16[1,1,512,4,128]{2,4,3,1,0:T(8,128)(2,1)}, u32[]{:S(2)}) copy-start(bf16[1,1,512,4,128]{2,4,3,1,0:T(8,128)(2,1)} %copy.179) | copy-start | bytes 1572868
  152.6 6.5 %copy-start.14 = (bf16[1,1,512,4,128]{2,4,3,1,0:T(8,128)(2,1)S(1)}, bf16[1,1,512,4,128]{2,4,3,1,0:T(8,128)(2,1)}, u32[]{:S(2)}) copy-start(bf16[1,1,512,4,128]{2,4,3,1,0:T(8,128)(2,1)} %copy.180) | copy-start | bytes 1572868
  152.7 6.5 %copy-start.15 = (bf16[1,1,512,4,128]{2,4,3,1,0:T(8,128)(2,1)S(1)}, bf16[1,1,512,4,128]{2,4,3,1,0:T(8,128)(2,1)}, u32[]{:S(2)}) copy-start(bf16[1,1,512,4,128]{2,4,3,1,0:T(8,128)(2,1)} %copy.181) | copy-start | bytes 1572868
  152.7 6.5 %copy-start.16 = (bf16[1,1,512,4,128]{2,4,3,1,0:T(8,128)(2,1)S(1)}, bf16[1,1,512,4,128]{2,4,3,1,0:T(8,128)(2,1)}, u32[]{:S(2)}) copy-start(bf16[1,1,512,4,128]{2,4,3,1,0:T(8,128)(2,1)} %copy.182) | copy-start | bytes 1572868
  152.7 6.5 %copy-start.17 = (bf16[1,1,512,4,128]{2,4,3,1,0:T(8,128)(2,1)S(1)}, bf16[1,1,512,4,128]{2,4,3,1,0:T(8,128)(2,1)}, u32[]{:S(2)}) copy-start(bf16[1,1,512,4,128]{2,4,3,1,0:T(8,128)(2,1)} %copy.183) | copy-start | bytes 1572868
  152.7 6.5 %copy-start.18 = (bf16[1,1,512,4,128]{2,4,3,1,0:T(8,128)(2,1)S(1)}, bf16[1,1,512,4,128]{2,4,3,1,0:T(8,128)(2,1)}, u32[]{:S(2)}) copy-start(bf16[1,1,512,4,128]{2,4,3,1,0:T(8,128)(2,1)} %copy.184) | copy-start | bytes 1572868
  164.5 16.1 %collective-permute-start.1 = (f32[2,512,1,128]{1,3,2,0:T(8,128)S(1)}, f32[2,512,1,128]{1,3,2,0:T(8,128)S(1)}, u32[]{:S(2)}, u32[]{:S(2)}) collective-permute-start(f32[2,512,1,128]{1,3,2,0:T(8,128)S(1)} %get-tuple-element.44), channel_id=1, source_target_pairs={{0,1},{1,2},{2,3},{3,4},{4,5},{5,6},{6,7},{7,8},{8,9},{9,10},{10,1... | collective-permute-start | bytes 1572872 | tf_op jit(solution)/shard_map/ppermute | solution.py:23
  166.4 14.2 %collective-permute-start.3 = (f32[2,512,1,128]{1,3,2,0:T(8,128)S(1)}, f32[2,512,1,128]{1,3,2,0:T(8,128)S(1)}, u32[]{:S(2)}, u32[]{:S(2)}) collective-permute-start(f32[2,512,1,128]{1,3,2,0:T(8,128)S(1)} %get-tuple-element.45), channel_id=1, source_target_pairs={{1,0},{2,1},{3,2},{4,3},{5,4},{6,5},{7,6},{8,7},{9,8},{10,9},{11,1... | collective-permute-start | bytes 1572872 | tf_op jit(solution)/shard_map/ppermute | solution.py:26
